TPU v7x, 32 devices: a whole 2x2x4 slice. The times are simulated.
32 devices in a mesh: dp: 8 (over z, x), tensor: 4 (over y, core).
Axes of the slice: x: 2, y: 2, z: 4, core: 2. Of those that a mesh axis runs over, the one named last changes fastest.
Arguments:
- inputs: bfloat16 [16, 1024, 768], P('dp'), may hold values from -6 to 6
- cotangent: bfloat16 [16, 1024, 768], P('dp', 'tensor'), may hold values from -6 to 6
- lengths: int32 [16], P('dp'), may hold values from 512 to 1024, as said below
- qkv_weight: bfloat16 [768, 3, 768], P(None, None, 'tensor'), may hold values from -0.21875 to 0.21875
- qkv_bias: bfloat16 [2, 768], P(None, 'tensor'), may hold values from -0.29882812 to 0.29882812
- out_weight: bfloat16 [768, 768], P('tensor'), may hold values from -4 to 4
- out_bias: bfloat16 [768], replicated, may hold values from -0.59765625 to 0.59765625
- first_gain: bfloat16 [768], replicated, may hold values from 0.5 to 1.5
- first_shift: bfloat16 [768], replicated, may hold values from -0.59765625 to 0.59765625
- up_weight: bfloat16 [768, 3072], P(None, 'tensor'), may hold values from -0.21875 to 0.21875
- up_bias: bfloat16 [3072], P('tensor'), may hold values from -0.59765625 to 0.59765625
- down_weight: bfloat16 [3072, 768], P('tensor'), may hold values from -0.109375 to 0.109375
- down_bias: bfloat16 [768], replicated, may hold values from -0.59765625 to 0.59765625
- second_gain: bfloat16 [768], replicated, may hold values from 0.5 to 1.5
- second_shift: bfloat16 [768], replicated, may hold values from -0.59765625 to 0.59765625
Outputs:
- outputs: bfloat16 [16, 1024, 768], P('dp', 'tensor')
- input_grad: bfloat16 [16, 1024, 768], P('dp', 'tensor')
- qkv_weight_grad: float32 [768, 3, 768], P('dp', None, 'tensor')
- qkv_bias_grad: float32 [2, 768], P(None, 'tensor')
- out_weight_grad: float32 [768, 768], P(('tensor', 'dp'))
- out_bias_grad: float32 [768], replicated
- first_gain_grad: float32 [768], replicated
- first_shift_grad: float32 [768], replicated
- up_weight_grad: float32 [768, 3072], P('dp', 'tensor')
- up_bias_grad: float32 [3072], P('tensor')
- down_weight_grad: float32 [3072, 768], P(('tensor', 'dp'))
- down_bias_grad: float32 [768], replicated
- second_gain_grad: float32 [768], replicated
- second_shift_grad: float32 [768], replicated
Inputs may be any that keep to these rules, and one draw needn't show every extreme that they name: `lengths`: each sequence has at least half of 1024 valid slots; in every draw some sequence has all 1024 slots valid and some has exactly half of 1024.
All inputs are finite; a program needn't handle non-finite values.
Results may differ from a plain program's by a relative error of at most 0.018.
Values may be sent and summed in bfloat16 or wider, within the bound.
No kernel may reach another device: no remote copies, remote signals or barrier semaphores. Data moves between devices by JAX's collectives and lax.ppermute only.
A program may use at most 192 MiB of HBM per device.

v0:
```python
import math
import jax
import jax.numpy as jnp
from jax import lax
from jax.sharding import PartitionSpec as P

HEAD = 64


def split_up(array, dim, peers):
    before, after = (array.shape[:dim], array.shape[dim + 1 :])
    return jnp.moveaxis(array.reshape(*before, peers, -1, *after), dim, 0)


def sent_and_summed(array, axis, dim):
    peers = lax.axis_size(axis)
    parts = lax.all_to_all(split_up(array, dim, peers), axis, 0, 0, tiled=True)
    return jnp.sum(parts.astype(jnp.float32), axis=0)


def in_one_piece(arrays, axis, dim, along):
    ends, at = ([], 0)
    for a in arrays[:-1]:
        at += a.shape[along]
        ends.append(at)
    both = jnp.concatenate(arrays, axis=along)
    return tuple(jnp.split(sent_and_summed(both, axis, dim), ends, axis=along))


def norm_rows(values, gain_row, shift_row):
    center = values - jnp.mean(values, axis=-1, keepdims=True)
    spread = jnp.mean(center * center, axis=-1, keepdims=True)
    return center * lax.rsqrt(spread + 1e-12) * gain_row + shift_row


def gelu_exact(values):
    return jax.nn.gelu(values, approximate=False)


def scores_for(query_part, key_rows, alive_cols):
    scores = jnp.einsum(
        "bhd,shd->hbs", query_part, key_rows, preferred_element_type=jnp.float32
    ) * (1.0 / math.sqrt(HEAD))
    return jnp.where(alive_cols[None, None, :], scores, -1e30)


def attend_forward(query_part, key_rows, value_rows, alive_cols):
    scores = scores_for(query_part, key_rows, alive_cols)
    row_max = jnp.max(scores, axis=-1, keepdims=True)
    exp_scores = jnp.exp(scores - row_max)
    row_total = jnp.sum(exp_scores, axis=-1, keepdims=True)
    soft_probs = (exp_scores / row_total).astype(jnp.bfloat16)
    context = jnp.einsum("hbs,shd->bhd", soft_probs, value_rows, preferred_element_type=jnp.float32)
    return (context, row_max + jnp.log(row_total))


def attend_backward(query_part, key_rows, value_rows, alive_cols, log_total, grad_context):
    scale = 1.0 / math.sqrt(HEAD)
    scores = scores_for(query_part, key_rows, alive_cols)
    soft_probs = jnp.exp(scores - log_total)
    probs_low = soft_probs.astype(jnp.bfloat16)
    grad_probs = jnp.einsum(
        "bhd,shd->hbs", grad_context, value_rows, preferred_element_type=jnp.float32
    )
    inner_sum = jnp.sum(soft_probs * grad_probs, axis=-1, keepdims=True)
    grad_scores = (soft_probs * (grad_probs - inner_sum)).astype(jnp.bfloat16)
    grad_query = (
        jnp.einsum("hbs,shd->bhd", grad_scores, key_rows, preferred_element_type=jnp.float32)
        * scale
    )
    grad_keys = (
        jnp.einsum("hbs,bhd->shd", grad_scores, query_part, preferred_element_type=jnp.float32)
        * scale
    )
    grad_values = jnp.einsum(
        "hbs,bhd->shd", probs_low, grad_context, preferred_element_type=jnp.float32
    )
    return (grad_query, grad_keys, grad_values)


def reduce_grads(groups):
    mat_grads, bias_grads, norm_grads = groups
    mat_sums = (
        sent_and_summed(mat_grads[0].astype(jnp.bfloat16), "dp", 0),
        sent_and_summed(mat_grads[1].astype(jnp.bfloat16), "dp", 0),
        *in_one_piece(
            (mat_grads[2].astype(jnp.bfloat16), mat_grads[3].astype(jnp.bfloat16)), "dp", 0, 1
        ),
    )
    bias_sums = lax.psum((bias_grads[0], bias_grads[1]), "dp")
    norm_sums = lax.psum(
        (norm_grads[0], norm_grads[1], norm_grads[2], norm_grads[3], norm_grads[4], norm_grads[5]),
        ("dp", "tensor"),
    )
    return (mat_sums, bias_sums, norm_sums)


def body(
    inputs,
    cotangent,
    lengths,
    qkv_weight,
    qkv_bias,
    out_weight,
    out_bias,
    first_gain,
    first_shift,
    up_weight,
    up_bias,
    down_weight,
    down_bias,
    second_gain,
    second_shift,
):
    seq_length = inputs.shape[1]
    local_width = out_weight.shape[0]
    local_heads = local_width // HEAD
    share_rows = cotangent.shape[1]
    block_rows = min(512, seq_length)
    row_start = lax.axis_index("tensor") * share_rows
    positions = jnp.arange(seq_length, dtype=jnp.int32)
    first_gain32 = first_gain.astype(jnp.float32)
    first_shift32 = first_shift.astype(jnp.float32)
    second_gain32 = second_gain.astype(jnp.float32)
    second_shift32 = second_shift.astype(jnp.float32)
    output_list = []
    input_list = []
    local_sum = None
    summed = None
    for micro_batch in range(inputs.shape[0]):
        tokens = inputs[micro_batch]
        alive_cols = positions < lengths[micro_batch]
        token_share = lax.dynamic_slice_in_dim(tokens, row_start, share_rows, 0).astype(jnp.float32)
        alive_share = lax.dynamic_slice_in_dim(alive_cols, row_start, share_rows, 0)
        projected = jnp.einsum(
            "sd,dkc->skc", tokens, qkv_weight, preferred_element_type=jnp.float32
        )
        query_rows = (
            (projected[:, 0] + qkv_bias[0])
            .astype(jnp.bfloat16)
            .reshape(seq_length, local_heads, HEAD)
        )
        key_rows = projected[:, 1].astype(jnp.bfloat16).reshape(seq_length, local_heads, HEAD)
        value_rows = (
            (projected[:, 2] + qkv_bias[1])
            .astype(jnp.bfloat16)
            .reshape(seq_length, local_heads, HEAD)
        )
        context_parts = []
        log_parts = []
        for block_start in range(0, seq_length, block_rows):
            context_part, log_part = attend_forward(
                query_rows[block_start : block_start + block_rows], key_rows, value_rows, alive_cols
            )
            context_parts.append(context_part)
            log_parts.append(log_part)
        context = (
            jnp.concatenate(context_parts, 0).reshape(seq_length, local_width).astype(jnp.bfloat16)
        )
        attention_share = lax.psum_scatter(
            jnp.dot(context, out_weight, preferred_element_type=jnp.float32).astype(jnp.bfloat16),
            "tensor",
            scatter_dimension=0,
            tiled=True,
        ).astype(jnp.float32)
        first_in = attention_share + out_bias + token_share
        first_norm, first_pull = jax.vjp(norm_rows, first_in, first_gain32, first_shift32)
        first_rows = lax.all_gather(first_norm.astype(jnp.bfloat16), "tensor", axis=0, tiled=True)
        hidden = jnp.dot(first_rows, up_weight, preferred_element_type=jnp.float32) + up_bias
        active = gelu_exact(hidden).astype(jnp.bfloat16)
        down_share = lax.psum_scatter(
            jnp.dot(active, down_weight, preferred_element_type=jnp.float32).astype(jnp.bfloat16),
            "tensor",
            scatter_dimension=0,
            tiled=True,
        ).astype(jnp.float32)
        second_in = down_share + down_bias + first_norm
        out_share, second_pull = jax.vjp(norm_rows, second_in, second_gain32, second_shift32)
        output_list.append(out_share.astype(jnp.bfloat16))
        seed_grad = jnp.where(alive_share[:, None], cotangent[micro_batch].astype(jnp.float32), 0.0)
        grad_second, grad_second_gain, grad_second_shift = second_pull(seed_grad)
        grad_down_rows = lax.all_gather(
            grad_second.astype(jnp.bfloat16), "tensor", axis=0, tiled=True
        )
        grad_active = lax.dot_general(
            grad_down_rows,
            down_weight,
            (((1,), (1,)), ((), ())),
            preferred_element_type=jnp.float32,
        )
        grad_down = lax.dot_general(
            active, grad_down_rows, (((0,), (0,)), ((), ())), preferred_element_type=jnp.float32
        )
        gelu_value, gelu_pull = jax.vjp(gelu_exact, hidden)
        grad_hidden = gelu_pull(grad_active)[0].astype(jnp.bfloat16)
        grad_up_bias = jnp.sum(grad_hidden, axis=0, dtype=jnp.float32)
        grad_up = lax.dot_general(
            first_rows, grad_hidden, (((0,), (0,)), ((), ())), preferred_element_type=jnp.float32
        )
        grad_first = (
            lax.psum_scatter(
                lax.dot_general(
                    grad_hidden,
                    up_weight,
                    (((1,), (1,)), ((), ())),
                    preferred_element_type=jnp.float32,
                ).astype(jnp.bfloat16),
                "tensor",
                scatter_dimension=0,
                tiled=True,
            ).astype(jnp.float32)
            + grad_second
        )
        grad_first_in, grad_first_gain, grad_first_shift = first_pull(grad_first)
        grad_attn_rows = lax.all_gather(
            grad_first_in.astype(jnp.bfloat16), "tensor", axis=0, tiled=True
        )
        grad_out = lax.dot_general(
            context, grad_attn_rows, (((0,), (0,)), ((), ())), preferred_element_type=jnp.float32
        )
        grad_context = lax.dot_general(
            grad_attn_rows, out_weight, (((1,), (1,)), ((), ())), preferred_element_type=jnp.float32
        )
        grad_context = grad_context.astype(jnp.bfloat16).reshape(seq_length, local_heads, HEAD)
        grad_keys = jnp.zeros((seq_length, local_heads, HEAD), jnp.float32)
        grad_values = jnp.zeros((seq_length, local_heads, HEAD), jnp.float32)
        query_grads = []
        for block_number, block_start in enumerate(range(0, seq_length, block_rows)):
            query_part_grad, key_part_grad, value_part_grad = attend_backward(
                query_rows[block_start : block_start + block_rows],
                key_rows,
                value_rows,
                alive_cols,
                log_parts[block_number],
                grad_context[block_start : block_start + block_rows],
            )
            query_grads.append(query_part_grad)
            grad_keys = grad_keys + key_part_grad
            grad_values = grad_values + value_part_grad
        grad_query = jnp.concatenate(query_grads, 0).reshape(seq_length, local_width)
        stacked = jnp.stack(
            [
                grad_query,
                grad_keys.reshape(seq_length, local_width),
                grad_values.reshape(seq_length, local_width),
            ],
            1,
        ).astype(jnp.bfloat16)
        grad_qkv = jnp.einsum("sd,skc->dkc", tokens, stacked, preferred_element_type=jnp.float32)
        grad_qkv_bias = jnp.stack(
            [
                jnp.sum(stacked[:, 0], axis=0, dtype=jnp.float32),
                jnp.sum(stacked[:, 2], axis=0, dtype=jnp.float32),
            ],
            0,
        )
        input_share = (
            lax.psum_scatter(
                jnp.einsum(
                    "skc,dkc->sd", stacked, qkv_weight, preferred_element_type=jnp.float32
                ).astype(jnp.bfloat16),
                "tensor",
                scatter_dimension=0,
                tiled=True,
            ).astype(jnp.float32)
            + grad_first_in
        )
        input_list.append(input_share.astype(jnp.bfloat16))
        micro_grads = (
            (grad_qkv, grad_out, grad_up, grad_down),
            (grad_qkv_bias, grad_up_bias),
            (
                jnp.sum(grad_first_in, axis=0),
                grad_first_gain,
                grad_first_shift,
                jnp.sum(grad_second, axis=0),
                grad_second_gain,
                grad_second_shift,
            ),
        )
        local_sum = (
            micro_grads if local_sum is None else jax.tree.map(jnp.add, local_sum, micro_grads)
        )
    summed = reduce_grads(local_sum)
    mat_sums, bias_sums, norm_sums = summed
    return (
        jnp.stack(output_list, 0),
        jnp.stack(input_list, 0),
        mat_sums[0],
        bias_sums[0],
        mat_sums[1],
        norm_sums[0],
        norm_sums[1],
        norm_sums[2],
        mat_sums[2],
        bias_sums[1],
        mat_sums[3],
        norm_sums[3],
        norm_sums[4],
        norm_sums[5],
    )


def solution(mesh):
    in_specs = (
        P("dp", None, None),
        P("dp", "tensor", None),
        P("dp"),
        P(None, None, "tensor"),
        P(None, "tensor"),
        P("tensor", None),
        P(),
        P(),
        P(),
        P(None, "tensor"),
        P("tensor"),
        P("tensor", None),
        P(),
        P(),
        P(),
    )
    out_specs = (
        P("dp", "tensor", None),
        P("dp", "tensor", None),
        P("dp", None, "tensor"),
        P(None, "tensor"),
        P(("tensor", "dp"), None),
        P(),
        P(),
        P(),
        P("dp", "tensor"),
        P("tensor"),
        P(("tensor", "dp"), None),
        P(),
        P(),
        P(),
    )
    return jax.shard_map(body, mesh=mesh, in_specs=in_specs, out_specs=out_specs, check_vma=False)
```

profile of v0, /device:TPU:0, one launch (start us, length us, event | category | flops | bytes accessed | tf_op | source)
XLA Modules:
  0.0 547.3 jit_solution(3790984775710877579)
XLA Ops:
  8.7 4.4 fusion.40
  45.8 3.3 fusion.132
  49.0 13.5 %reduce-scatter.9.cloned.1.call-done = bf16[256,768]{1,0:T(8,128)(2,1)} async-done(((bf16[1024,768]{1,0:T(8,128)(2,1)}), bf16[256,768]{1,0:T(8,128)(2,1)}) %reduce-scatter.9.cloned.1.call-update) | async-done | bytes 393232 | tf_op jit(solution)/shard_map/reduce_scatter | solution.py:160
  62.5 30.9 %reduce-scatter.13.cloned.1.call-done = bf16[256,768]{1,0:T(8,128)(2,1)} async-done(((bf16[1024,768]{1,0:T(8,128)(2,1)}), bf16[256,768]{1,0:T(8,128)(2,1)}) %reduce-scatter.13.cloned.1.call-update) | async-done | bytes 393232 | tf_op jit(solution)/shard_map/reduce_scatter | solution.py:160
  101.9 17.7 %all-gather.9.cloned.1.call-done = bf16[1024,768]{1,0:T(8,128)(2,1)} async-done(((bf16[256,768]{1,0:T(8,128)(2,1)}), bf16[1024,768]{1,0:T(8,128)(2,1)}) %all-gather.9.cloned.1.call-update) | async-done | bytes 1572880 | tf_op jit(solution)/shard_map/all_gather | solution.py:168
  119.5 4.4 fusion.143
  124.0 17.2 %all-gather.7.cloned.1.call-done = bf16[1024,768]{1,0:T(8,128)(2,1)} async-done(((bf16[256,768]{1,0:T(8,128)(2,1)}), bf16[1024,768]{1,0:T(8,128)(2,1)}) %all-gather.7.cloned.1.call-update) | async-done | bytes 1572880 | tf_op jit(solution)/shard_map/all_gather | solution.py:168
  141.2 17.4 %multiply_convert_fusion.5 = (bf16[1024,768]{1,0:T(8,128)(2,1)S(1)}, f32[1024,768]{1,0:T(8,128)}, bf16[1024,768]{1,0:T(8,128)(2,1)}, f32[1024,768]{1,0:T(8,128)}, f32[1024,768]{1,0:T(8,128)}) fusion(f32[768]{0:T(1024)} %convert_element_type.280, f32[1024,768]{1,0:T(8,128)} %fusion.143, bf16[1024,768]{1,0:T(8,128)(2,1)} %all-gather.7.cloned.1.call-done, ...), kind=kOutput, calls=%fused_computation.64 | convolution fusion | flops 1311768576 | bytes 18484224 | tf_op jit(solution)/shard_map/dot_general | solution.py:169
  162.4 4.3 convolution_convert_fusion.2
  173.1 17.5 %reduce-scatter.11.cloned.1.call-done = bf16[256,768]{1,0:T(8,128)(2,1)} async-done(((bf16[1024,768]{1,0:T(8,128)(2,1)}), bf16[256,768]{1,0:T(8,128)(2,1)}) %reduce-scatter.11.cloned.1.call-update) | async-done | bytes 393232 | tf_op jit(solution)/shard_map/reduce_scatter | solution.py:171
  190.7 30.8 %reduce-scatter.15.cloned.1.call-done = bf16[256,768]{1,0:T(8,128)(2,1)} async-done(((bf16[1024,768]{1,0:T(8,128)(2,1)}), bf16[256,768]{1,0:T(8,128)(2,1)}) %reduce-scatter.15.cloned.1.call-update) | async-done | bytes 393232 | tf_op jit(solution)/shard_map/reduce_scatter | solution.py:171
  231.8 17.1 %all-gather.11.cloned.1.call-done = bf16[1024,768]{1,0:T(8,128)(2,1)} async-done(((bf16[256,768]{1,0:T(8,128)(2,1)}), bf16[1024,768]{1,0:T(8,128)(2,1)}) %all-gather.11.cloned.1.call-update) | async-done | bytes 1572880 | tf_op jit(solution)/shard_map/all_gather | solution.py:182
  248.9 4.8 fusion.144
  253.7 17.0 %all-gather.15.cloned.1.call-done = bf16[1024,768]{1,0:T(8,128)(2,1)} async-done(((bf16[256,768]{1,0:T(8,128)(2,1)}), bf16[1024,768]{1,0:T(8,128)(2,1)}) %all-gather.15.cloned.1.call-update) | async-done | bytes 1572880 | tf_op jit(solution)/shard_map/all_gather | solution.py:182
  270.7 11.5 %convert_reduce_fusion.1 = (f32[768]{0:T(1024)}, bf16[1024,768]{1,0:T(8,128)(2,1)}, f32[768]{0:T(1024)}, bf16[1024,768]{1,0:T(8,128)(2,1)S(1)}) fusion(f32[1024,768]{1,0:T(8,128)} %get-tuple-element.108, f32[1024,768]{1,0:T(8,128)} %fusion.143, f32[768]{0:T(1024)} %convert_element_type.280, f32[1024,768]{1,0:T(8,128)} %fusion.144, ...), kind=kOutput, calls=%fused_computation.43 | convolution fusion | flops 1234696704 | bytes 21636096 | tf_op jit(solution)/shard_map/dot_general | solution.py:185
  286.1 4.0 convolution_convert_fusion
  295.0 4.8 fusion.149
  299.9 14.5 %reduce-scatter.17.cloned.1.call-done = bf16[256,768]{1,0:T(8,128)(2,1)} async-done(((bf16[1024,768]{1,0:T(8,128)(2,1)}), bf16[256,768]{1,0:T(8,128)(2,1)}) %reduce-scatter.17.cloned.1.call-update) | async-done | bytes 393232 | tf_op jit(solution)/shard_map/reduce_scatter | solution.py:201
  314.4 30.7 %reduce-scatter.21.cloned.1.call-done = bf16[256,768]{1,0:T(8,128)(2,1)} async-done(((bf16[1024,768]{1,0:T(8,128)(2,1)}), bf16[256,768]{1,0:T(8,128)(2,1)}) %reduce-scatter.21.cloned.1.call-update) | async-done | bytes 393232 | tf_op jit(solution)/shard_map/reduce_scatter | solution.py:201
  345.2 3.1 multiply_reduce_fusion.5
  352.2 3.5 fusion.148
  360.7 4.3 copy.32
  365.0 5.6 %all-to-all-start.2 = ((bf16[8,96,1536]{2,1,0:T(8,128)(2,1)}), bf16[8,96,1536]{2,1,0:T(8,128)(2,1)}, u32[]{:S(2)}, u32[]{:S(2)}) async-start(bf16[8,96,1536]{2,1,0:T(8,128)(2,1)} %bitcast.251), calls=%async_computation.10 | async-start | bytes 4718592 | tf_op jit(solution)/shard_map/all_to_all | solution.py:17
  376.5 3.9 multiply_reduce_fusion.3
  387.5 4.2 multiply_reduce_fusion.2
  397.3 4.1 fusion.62
  401.9 3.5 multiply_convert_fusion.2
  411.3 3.9 multiply_reduce_fusion.1
  434.6 5.8 %all-to-all-start.1 = ((bf16[8,24,768]{2,1,0:T(8,128)(2,1)}), bf16[8,24,768]{2,1,0:T(8,128)(2,1)}, u32[]{:S(2)}, u32[]{:S(2)}) async-start(bf16[8,24,768]{2,1,0:T(8,128)(2,1)} %bitcast.292), calls=%async_computation.9 | async-start | bytes 589824 | tf_op jit(solution)/shard_map/all_to_all | solution.py:17
  450.4 5.0 all-to-all-start
  457.6 45.9 %all-reduce = (f32[768]{0:T(1024)}, f32[768]{0:T(1024)}, f32[768]{0:T(1024)}, f32[768]{0:T(1024)}, f32[768]{0:T(1024)}, /*index=5*/f32[768]{0:T(1024)}) all-reduce(f32[768]{0:T(1024)S(1)} %add.359, f32[768]{0:T(1024)S(1)} %add.360, f32[768]{0:T(1024)S(1)} %add.361, ...), channel_id=1, replica_groups=mesh['dp'=8,'tensor'=4] {'dp','tensor'}, use_global_device_ids=true, to_apply=%region_45.46 | all-reduce | flops 4608 | bytes 36864 | tf_op jit(solution)/shard_map/psum | solution.py:91
  510.9 22.0 %all-reduce.1 = (f32[2,192]{1,0:T(2,128)}, f32[768]{0:T(1024)}) all-reduce(f32[2,192]{1,0:T(2,128)S(1)} %maximum_add_fusion, f32[768]{0:T(1024)S(1)} %add.364), channel_id=1, replica_groups=mesh['dp'=8,'tensor'=4] {'dp'}, use_global_device_ids=true, to_apply=%region_41.42 | all-reduce | flops 1152 | bytes 9216 | tf_op jit(solution)/shard_map/psum | solution.py:90
  (423 shorter events, 150.4 us)
Async XLA Ops:
  7.2 112.4 %copy-start = (bf16[768,768]{1,0:T(8,128)(2,1)S(1)}, bf16[768,768]{1,0:T(8,128)(2,1)}, u32[]{:S(2)}) copy-start(bf16[768,768]{1,0:T(8,128)(2,1)} %param.24) | copy-start | bytes 3538948
  7.2 55.3 %reduce-scatter.9.cloned.1.call-start = ((), (), s32[]{:S(2)}) async-start(), calls=%async_computation.11 | async-start | bytes 1966080 | tf_op jit(solution)/shard_map/reduce_scatter | solution.py:160
  19.8 13.8 %copy-start.28 = (bf16[512,192]{0,1:T(8,128)(2,1)}, bf16[512,192]{0,1:T(8,128)(2,1)S(1)}, u32[]{:S(2)}) copy-start(bf16[512,192]{0,1:T(8,128)(2,1)S(1)} %get-tuple-element.98) | copy-start | bytes 589828
  19.8 16.5 %copy-start.32 = (bf16[512,192]{0,1:T(8,128)(2,1)}, bf16[512,192]{0,1:T(8,128)(2,1)S(1)}, u32[]{:S(2)}) copy-start(bf16[512,192]{0,1:T(8,128)(2,1)S(1)} %get-tuple-element.97) | copy-start | bytes 589828
  23.9 16.8 %copy-start.15 = (bf16[1024,3,64]{0,2,1:T(8,128)(2,1)}, bf16[1024,3,64]{0,2,1:T(8,128)(2,1)S(1)}, u32[]{:S(2)}) copy-start(bf16[1024,3,64]{0,2,1:T(8,128)(2,1)S(1)} %get-tuple-element.109) | copy-start | bytes 1179652
  31.5 61.9 %reduce-scatter.13.cloned.1.call-start = ((), (), s32[]{:S(2)}) async-start(), calls=%async_computation.14 | async-start | bytes 1966080 | tf_op jit(solution)/shard_map/reduce_scatter | solution.py:160
  45.1 74.5 %all-gather.9.cloned.1.call-start = ((), (), s32[]{:S(2)}) async-start(), calls=%async_computation.15 | async-start | bytes 1966080 | tf_op jit(solution)/shard_map/all_gather | solution.py:168
  49.0 172.4 %copy-start.12 = (bf16[1,1024,768]{2,1,0:T(8,128)(2,1)}, bf16[1,1024,768]{2,1,0:T(8,128)(2,1)S(1)}, u32[]{:S(2)}) copy-start(bf16[1,1024,768]{2,1,0:T(8,128)(2,1)S(1)} %get-tuple-element.80) | copy-start | bytes 4718596
  62.5 34.8 %copy-start.7 = (bf16[256,768]{1,0:T(8,128)(2,1)S(1)}, bf16[256,768]{1,0:T(8,128)(2,1)}, u32[]{:S(2)}) copy-start(bf16[256,768]{1,0:T(8,128)(2,1)} %reduce-scatter.9.cloned.1.call-done) | copy-start | bytes 1179652
  99.7 41.5 %all-gather.7.cloned.1.call-start = ((), (), s32[]{:S(2)}) async-start(), calls=%async_computation.12 | async-start | bytes 1966080 | tf_op jit(solution)/shard_map/all_gather | solution.py:168
  100.3 90.4 %reduce-scatter.11.cloned.1.call-start = ((), (), s32[]{:S(2)}) async-start(), calls=%async_computation.13 | async-start | bytes 1966080 | tf_op jit(solution)/shard_map/reduce_scatter | solution.py:171
  141.2 18.6 %copy-start.111 = (bf16[768,768]{1,0:T(8,128)(2,1)S(1)}, bf16[768,768]{1,0:T(8,128)(2,1)}, u32[]{:S(2)}) copy-start(bf16[768,768]{1,0:T(8,128)(2,1)} %param.26) | copy-start | bytes 3538948
  162.4 59.1 %reduce-scatter.15.cloned.1.call-start = ((), (), s32[]{:S(2)}) async-start(), calls=%async_computation.16 | async-start | bytes 1966080 | tf_op jit(solution)/shard_map/reduce_scatter | solution.py:171
  166.7 82.2 %all-gather.11.cloned.1.call-start = ((), (), s32[]{:S(2)}) async-start(), calls=%async_computation.17 | async-start | bytes 1966080 | tf_op jit(solution)/shard_map/all_gather | solution.py:182
  229.1 41.6 %all-gather.15.cloned.1.call-start = ((), (), s32[]{:S(2)}) async-start(), calls=%async_computation.21 | async-start | bytes 1966080 | tf_op jit(solution)/shard_map/all_gather | solution.py:182
  231.3 83.1 %reduce-scatter.17.cloned.1.call-start = ((), (), s32[]{:S(2)}) async-start(), calls=%async_computation.18 | async-start | bytes 1966080 | tf_op jit(solution)/shard_map/reduce_scatter | solution.py:201
  286.1 59.1 %reduce-scatter.21.cloned.1.call-start = ((), (), s32[]{:S(2)}) async-start(), calls=%async_computation.22 | async-start | bytes 1966080 | tf_op jit(solution)/shard_map/reduce_scatter | solution.py:201
  290.1 84.1 %all-gather.13.cloned.1.call-start = ((), (), s32[]{:S(2)}) async-start(), calls=%async_computation.19 | async-start | bytes 1966080 | tf_op jit(solution)/shard_map/all_gather | solution.py:215
  365.0 69.6 %all-to-all-start.2 = ((bf16[8,96,1536]{2,1,0:T(8,128)(2,1)}), bf16[8,96,1536]{2,1,0:T(8,128)(2,1)}, u32[]{:S(2)}, u32[]{:S(2)}) async-start(bf16[8,96,1536]{2,1,0:T(8,128)(2,1)} %bitcast.251), calls=%async_computation.10 | async-start | bytes 4718592 | tf_op jit(solution)/shard_map/all_to_all | solution.py:17
  370.7 23.8 %all-gather.17.cloned.1.call-start = ((), (), s32[]{:S(2)}) async-start(), calls=%async_computation.23 | async-start | bytes 1966080 | tf_op jit(solution)/shard_map/all_gather | solution.py:215
  374.0 162.9 %reduce-scatter.19.cloned.1.call-start = ((), (), s32[]{:S(2)}) async-start(), calls=%async_computation.20 | async-start | bytes 1966080 | tf_op jit(solution)/shard_map/reduce_scatter | solution.py:258
  410.9 127.2 %reduce-scatter.23.cloned.1.call-start = ((), (), s32[]{:S(2)}) async-start(), calls=%async_computation.24 | async-start | bytes 1966080 | tf_op jit(solution)/shard_map/reduce_scatter | solution.py:258
  434.6 15.9 %all-to-all-start.1 = ((bf16[8,24,768]{2,1,0:T(8,128)(2,1)}), bf16[8,24,768]{2,1,0:T(8,128)(2,1)}, u32[]{:S(2)}, u32[]{:S(2)}) async-start(bf16[8,24,768]{2,1,0:T(8,128)(2,1)} %bitcast.292), calls=%async_computation.9 | async-start | bytes 589824 | tf_op jit(solution)/shard_map/all_to_all | solution.py:17
  445.4 10.0 %copy-start.76 = (f32[768]{0:T(1024)S(1)}, f32[768]{0:T(1024)}, u32[]{:S(2)}) copy-start(f32[768]{0:T(1024)} %get-tuple-element.34) | copy-start | bytes 9220
  445.4 10.0 %copy-start.77 = (f32[768]{0:T(1024)S(1)}, f32[768]{0:T(1024)}, u32[]{:S(2)}) copy-start(f32[768]{0:T(1024)} %get-tuple-element.39) | copy-start | bytes 9220
  445.4 10.0 %copy-start.74 = (f32[768]{0:T(1024)S(1)}, f32[768]{0:T(1024)}, u32[]{:S(2)}) copy-start(f32[768]{0:T(1024)} %get-tuple-element.42) | copy-start | bytes 9220
  445.4 10.0 %copy-start.75 = (f32[768]{0:T(1024)S(1)}, f32[768]{0:T(1024)}, u32[]{:S(2)}) copy-start(f32[768]{0:T(1024)} %get-tuple-element.43) | copy-start | bytes 9220
  445.4 10.0 %copy-start.49 = (bf16[1,256,768]{2,1,0:T(8,128)(2,1)S(1)}, bf16[1,256,768]{2,1,0:T(8,128)(2,1)}, u32[]{:S(2)}) copy-start(bf16[1,256,768]{2,1,0:T(8,128)(2,1)} %get-tuple-element.83) | copy-start | bytes 1179652
  450.4 84.1 %all-to-all-start = ((bf16[8,96,3,192]{1,3,2,0:T(8,128)(2,1)}), bf16[8,96,3,192]{1,3,2,0:T(8,128)(2,1)}, u32[]{:S(2)}, u32[]{:S(2)}) async-start(bf16[8,96,3,192]{1,3,2,0:T(8,128)(2,1)} %copy.30), calls=%async_computation.8 | async-start | bytes 2359296 | tf_op jit(solution)/shard_map/all_to_all | solution.py:17
  505.5 31.4 %copy-start.14 = (f32[256,768]{1,0:T(8,128)S(1)}, f32[256,768]{1,0:T(8,128)}, u32[]{:S(2)}) copy-start(f32[256,768]{1,0:T(8,128)} %copy-done.13) | copy-start | bytes 2359300
  505.5 31.4 %copy-start.95 = (f32[256]{0:T(256)S(1)}, f32[256]{0:T(256)}, u32[]{:S(2)}) copy-start(f32[256]{0:T(256)} %copy-done.94) | copy-start | bytes 3076
  505.5 32.6 %copy-start.97 = (f32[256]{0:T(256)S(1)}, f32[256]{0:T(256)}, u32[]{:S(2)}) copy-start(f32[256]{0:T(256)} %copy-done.96) | copy-start | bytes 3076
  (113 other events, 384.7 us)
Sparse Core Ops, SparseCore 0:
  31.6 30.8 reduce-scatter.8
  65.2 28.1 reduce-scatter.12
  99.8 19.6 all-gather.8
  121.5 19.6 all-gather.6
  162.5 28.1 reduce-scatter.10
  193.2 28.1 reduce-scatter.14
  229.2 19.6 all-gather.10
  251.0 19.6 all-gather.14
  286.2 28.1 reduce-scatter.16
  316.9 28.1 reduce-scatter.20
  352.3 19.6 all-gather.12
  374.1 20.2 all-gather.16
  411.0 28.1 reduce-scatter.18
  441.8 28.6 reduce-scatter.22
where the time goes:
time: 556 us; the launch traced here: 547 us
  waiting for transfers between devices  212 us (38%)
  matrix products  131 us (24%)
  other arithmetic  68.8 us (12%)
  blocking collectives  67.8 us (12%)
  local copies, waits for them, and re-layouts  33.1 us (6%)
  starting transfers between devices  18.6 us (3%)
  between operations  16.2 us (3%)
    reduce_scatter x2, waiting for transfers between devices, body(): lax.psum_scatter(jnp.dot(active, down_weight, preferred_element_type=jnp....  48.3 us
    psum x1, blocking collectives, reduce_grads(): lax.psum((norm_grads[0], norm_grads[1], norm_grads[2], norm_grads[3], nor...  45.9 us
    reduce_scatter x2, waiting for transfers between devices, body(): lax.psum_scatter(lax.dot_general(grad_hidden, up_weight, (((1,), (1,)), (...  45.3 us
    reduce_scatter x2, waiting for transfers between devices, body(): lax.psum_scatter(jnp.dot(context, out_weight, preferred_element_type=jnp....  44.3 us
    all_gather x2, waiting for transfers between devices, body(): lax.all_gather(first_norm.astype(jnp.bfloat16), 'tensor', axis=0, tiled=T...  34.9 us
    all_gather x2, waiting for transfers between devices, body(): lax.all_gather(grad_second.astype(jnp.bfloat16), 'tensor', axis=0, tiled=...  34.1 us
    psum x1, blocking collectives, reduce_grads(): bias_sums = lax.psum((bias_grads[0], bias_grads[1]), 'dp')  22 us
    dot_general x2, matrix products, body(): jnp.dot(first_rows, up_weight, preferred_element_type=jnp.float32) + up_bias  21.8 us
  transfers between devices with their start and end apart: 17, of which 12 were waited for; matrix products, arithmetic and copies ran while one was open for 26% of the time, Pallas kernels for 0%

commit v1 on v0

--- a/solution.py
+++ b/solution.py
@@ -179,9 +179,25 @@
         output_list.append(out_share.astype(jnp.bfloat16))
         seed_grad = jnp.where(alive_share[:, None], cotangent[micro_batch].astype(jnp.float32), 0.0)
         grad_second, grad_second_gain, grad_second_shift = second_pull(seed_grad)
-        grad_down_rows = lax.all_gather(
-            grad_second.astype(jnp.bfloat16), "tensor", axis=0, tiled=True
-        )
+        shard = grad_second.astype(jnp.bfloat16)
+        size, mine, rows = (lax.axis_size("tensor"), lax.axis_index("tensor"), shard.shape[0])
+        right = [(i, (i + 1) % size) for i in range(size)]
+        behind = [(i, (i - 1) % size) for i in range(size)]
+        out = jnp.zeros((*shard.shape[:0], size * rows, *shard.shape[0 + 1 :]), shard.dtype)
+        out = lax.dynamic_update_slice_in_dim(out, shard, mine * rows, axis=0)
+        from_left = from_right = shard
+        half = size // 2
+        for turn in range(1, half + 1):
+            from_left = lax.ppermute(from_left, "tensor", right)
+            out = lax.dynamic_update_slice_in_dim(
+                out, from_left, (mine - turn) % size * rows, axis=0
+            )
+            if turn < size - half:
+                from_right = lax.ppermute(from_right, "tensor", behind)
+                out = lax.dynamic_update_slice_in_dim(
+                    out, from_right, (mine + turn) % size * rows, axis=0
+                )
+        grad_down_rows = out
         grad_active = lax.dot_general(
             grad_down_rows,
             down_weight,

time: 556 us -> 543 us (0.977)
  waiting for transfers between devices: 212 us -> 191 us
  local copies, waits for them, and re-layouts: 33.1 us -> 43.8 us
    all_gather x2 -> x0, waiting for transfers between devices: 34.1 us -> none  [body(): lax.all_gather(grad_second.astype(jnp.bfloat16), 'tensor', axis=0, tiled=...]
    ppermute x0 -> x6, waiting for transfers between devices: none -> 12.6 us  [the longest x4 12.6 us: body(): from_left = lax.ppermute(from_left, 'tensor', right)]
    dynamic_update_slice x0 -> x6, local copies, waits for them, and re-layouts: none -> 8.7 us  [the longest x4 5.13 us: body(): lax.dynamic_update_slice_in_dim(out, from_left, (mine - turn) % size * ro...]
    dot_general x2, matrix products: 16.3 us -> 10.2 us  [body(): lax.dot_general(grad_down_rows, down_weight, (((1,), (1,)), ((), ())), pr...]
    unnamed x257 -> x267, local copies, waits for them, and re-layouts: 14.6 us -> 14 us
  transfers between devices with their start and end apart: 17 -> 21, of which waited for: 12 -> 13; matrix products, arithmetic and copies ran while one was open for 26% -> 28% of each run, Pallas kernels for 0% -> 0%
where the time goes in v1:
time: 543 us; the launch traced here: 534 us
  waiting for transfers between devices  191 us (35%)
  matrix products  127 us (23%)
  other arithmetic  67.9 us (13%)
  blocking collectives  67.9 us (13%)
  local copies, waits for them, and re-layouts  43.8 us (8%)
  starting transfers between devices  20.5 us (4%)
  between operations  16.2 us (3%)
    reduce_scatter x2, waiting for transfers between devices, body(): lax.psum_scatter(jnp.dot(active, down_weight, preferred_element_type=jnp....  48.2 us
    reduce_scatter x2, waiting for transfers between devices, body(): lax.psum_scatter(lax.dot_general(grad_hidden, up_weight, (((1,), (1,)), (...  46.9 us
    psum x1, blocking collectives, reduce_grads(): lax.psum((norm_grads[0], norm_grads[1], norm_grads[2], norm_grads[3], nor...  45.9 us
    reduce_scatter x2, waiting for transfers between devices, body(): lax.psum_scatter(jnp.dot(context, out_weight, preferred_element_type=jnp....  44.3 us
    all_gather x2, waiting for transfers between devices, body(): lax.all_gather(first_norm.astype(jnp.bfloat16), 'tensor', axis=0, tiled=T...  34.7 us
    psum x1, blocking collectives, reduce_grads(): bias_sums = lax.psum((bias_grads[0], bias_grads[1]), 'dp')  22 us
    dot_general x2, matrix products, body(): jnp.dot(first_rows, up_weight, preferred_element_type=jnp.float32) + up_bias  21.9 us
    all_to_all x3, starting transfers between devices, sent_and_summed(): parts = lax.all_to_all(split_up(array, dim, peers), axis, 0, 0, tiled=True)  16.2 us
  transfers between devices with their start and end apart: 21, of which 13 were waited for; matrix products, arithmetic and copies ran while one was open for 28% of the time, Pallas kernels for 0%

profile of v1, /device:TPU:0, one launch (start us, length us, event | category | flops | bytes accessed | tf_op | source)
XLA Modules:
  0.0 534.2 jit_solution(17178654032528646017)
XLA Ops:
  8.7 4.3 fusion.40
  45.8 3.2 fusion.132
  49.1 13.4 %reduce-scatter.9.cloned.1.call-done = bf16[256,768]{1,0:T(8,128)(2,1)} async-done(((bf16[1024,768]{1,0:T(8,128)(2,1)}), bf16[256,768]{1,0:T(8,128)(2,1)}) %reduce-scatter.9.cloned.1.call-update) | async-done | bytes 393232 | tf_op jit(solution)/shard_map/reduce_scatter | solution.py:160
  62.5 30.9 %reduce-scatter.13.cloned.1.call-done = bf16[256,768]{1,0:T(8,128)(2,1)} async-done(((bf16[1024,768]{1,0:T(8,128)(2,1)}), bf16[256,768]{1,0:T(8,128)(2,1)}) %reduce-scatter.13.cloned.1.call-update) | async-done | bytes 393232 | tf_op jit(solution)/shard_map/reduce_scatter | solution.py:160
  102.1 17.4 %all-gather.7.cloned.1.call-done = bf16[1024,768]{1,0:T(8,128)(2,1)} async-done(((bf16[256,768]{1,0:T(8,128)(2,1)}), bf16[1024,768]{1,0:T(8,128)(2,1)}) %all-gather.7.cloned.1.call-update) | async-done | bytes 1572880 | tf_op jit(solution)/shard_map/all_gather | solution.py:168
  119.5 4.4 fusion.143
  123.9 17.3 %all-gather.5.cloned.1.call-done = bf16[1024,768]{1,0:T(8,128)(2,1)} async-done(((bf16[256,768]{1,0:T(8,128)(2,1)}), bf16[1024,768]{1,0:T(8,128)(2,1)}) %all-gather.5.cloned.1.call-update) | async-done | bytes 1572880 | tf_op jit(solution)/shard_map/all_gather | solution.py:168
  141.2 17.4 %multiply_convert_fusion.5 = (bf16[1024,768]{1,0:T(8,128)(2,1)S(1)}, f32[1024,768]{1,0:T(8,128)}, bf16[1024,768]{1,0:T(8,128)(2,1)}, f32[1024,768]{1,0:T(8,128)}, f32[1024,768]{1,0:T(8,128)}) fusion(f32[768]{0:T(1024)} %convert_element_type.280, f32[1024,768]{1,0:T(8,128)} %fusion.143, bf16[1024,768]{1,0:T(8,128)(2,1)} %all-gather.5.cloned.1.call-done, ...), kind=kOutput, calls=%fused_computation.64 | convolution fusion | flops 1311768576 | bytes 18484224 | tf_op jit(solution)/shard_map/dot_general | solution.py:169
  162.4 4.4 convolution_convert_fusion.2
  173.2 17.5 %reduce-scatter.11.cloned.1.call-done = bf16[256,768]{1,0:T(8,128)(2,1)} async-done(((bf16[1024,768]{1,0:T(8,128)(2,1)}), bf16[256,768]{1,0:T(8,128)(2,1)}) %reduce-scatter.11.cloned.1.call-update) | async-done | bytes 393232 | tf_op jit(solution)/shard_map/reduce_scatter | solution.py:171
  190.7 30.8 %reduce-scatter.15.cloned.1.call-done = bf16[256,768]{1,0:T(8,128)(2,1)} async-done(((bf16[1024,768]{1,0:T(8,128)(2,1)}), bf16[256,768]{1,0:T(8,128)(2,1)}) %reduce-scatter.15.cloned.1.call-update) | async-done | bytes 393232 | tf_op jit(solution)/shard_map/reduce_scatter | solution.py:171
  234.1 4.0 collective-permute-done
  238.1 8.4 %collective-permute-done.3 = bf16[256,768]{1,0:T(8,128)(2,1)} collective-permute-done((bf16[256,768]{1,0:T(8,128)(2,1)}, bf16[256,768]{1,0:T(8,128)(2,1)}, u32[]{:S(2)}, u32[]{:S(2)}) %collective-permute-start.3) | collective-permute-done | bytes 393248 | tf_op jit(solution)/shard_map/ppermute | solution.py:191
  254.6 3.2 fusion.144
  259.4 7.1 %convert_reduce_fusion.1 = (f32[768]{0:T(1024)}, bf16[1024,768]{1,0:T(8,128)(2,1)}, f32[768]{0:T(1024)}, bf16[1024,768]{1,0:T(8,128)(2,1)S(1)}) fusion(f32[1024,768]{1,0:T(8,128)S(1)} %copy-done.123, f32[1024,768]{1,0:T(8,128)S(1)} %copy-done.116, f32[768]{0:T(1024)S(1)} %copy-done.102, f32[1024,768]{1,0:T(8,128)S(1)} %fusion.144, ...), kind=kOutput, calls=%fused_computation.43 | convolution fusion | flops 1234696704 | bytes 21636096 | tf_op jit(solution)/shard_map/dot_general | solution.py:201
  270.4 4.0 convolution_convert_fusion
  279.1 5.0 fusion.149
  284.1 16.0 %reduce-scatter.17.cloned.1.call-done = bf16[256,768]{1,0:T(8,128)(2,1)} async-done(((bf16[1024,768]{1,0:T(8,128)(2,1)}), bf16[256,768]{1,0:T(8,128)(2,1)}) %reduce-scatter.17.cloned.1.call-update) | async-done | bytes 393232 | tf_op jit(solution)/shard_map/reduce_scatter | solution.py:217
  300.1 30.9 %reduce-scatter.21.cloned.1.call-done = bf16[256,768]{1,0:T(8,128)(2,1)} async-done(((bf16[1024,768]{1,0:T(8,128)(2,1)}), bf16[256,768]{1,0:T(8,128)(2,1)}) %reduce-scatter.21.cloned.1.call-update) | async-done | bytes 393232 | tf_op jit(solution)/shard_map/reduce_scatter | solution.py:217
  331.0 3.1 multiply_reduce_fusion.5
  338.1 3.5 fusion.148
  347.7 4.3 copy.32
  352.0 5.6 %all-to-all-start.2 = ((bf16[8,96,1536]{2,1,0:T(8,128)(2,1)}), bf16[8,96,1536]{2,1,0:T(8,128)(2,1)}, u32[]{:S(2)}, u32[]{:S(2)}) async-start(bf16[8,96,1536]{2,1,0:T(8,128)(2,1)} %bitcast.251), calls=%async_computation.10 | async-start | bytes 4718592 | tf_op jit(solution)/shard_map/all_to_all | solution.py:17
  363.5 3.9 multiply_reduce_fusion.3
  374.6 4.2 multiply_reduce_fusion.2
  384.2 4.1 fusion.62
  388.8 3.5 multiply_convert_fusion.2
  398.3 3.9 multiply_reduce_fusion.1
  421.7 5.7 %all-to-all-start.1 = ((bf16[8,24,768]{2,1,0:T(8,128)(2,1)}), bf16[8,24,768]{2,1,0:T(8,128)(2,1)}, u32[]{:S(2)}, u32[]{:S(2)}) async-start(bf16[8,24,768]{2,1,0:T(8,128)(2,1)} %bitcast.292), calls=%async_computation.9 | async-start | bytes 589824 | tf_op jit(solution)/shard_map/all_to_all | solution.py:17
  437.4 4.8 all-to-all-start
  444.4 45.9 %all-reduce = (f32[768]{0:T(1024)}, f32[768]{0:T(1024)}, f32[768]{0:T(1024)}, f32[768]{0:T(1024)}, f32[768]{0:T(1024)}, /*index=5*/f32[768]{0:T(1024)}) all-reduce(f32[768]{0:T(1024)S(1)} %add.399, f32[768]{0:T(1024)S(1)} %add.400, f32[768]{0:T(1024)S(1)} %add.401, ...), channel_id=1, replica_groups=mesh['dp'=8,'tensor'=4] {'dp','tensor'}, use_global_device_ids=true, to_apply=%region_45.46 | all-reduce | flops 4608 | bytes 36864 | tf_op jit(solution)/shard_map/psum | solution.py:91
  497.8 22.0 %all-reduce.1 = (f32[2,192]{1,0:T(2,128)}, f32[768]{0:T(1024)}) all-reduce(f32[2,192]{1,0:T(2,128)S(1)} %maximum_add_fusion, f32[768]{0:T(1024)S(1)} %add.404), channel_id=1, replica_groups=mesh['dp'=8,'tensor'=4] {'dp'}, use_global_device_ids=true, to_apply=%region_41.42 | all-reduce | flops 1152 | bytes 9216 | tf_op jit(solution)/shard_map/psum | solution.py:90
  (447 shorter events, 163.8 us)
Async XLA Ops:
  7.2 112.3 %copy-start = (bf16[768,768]{1,0:T(8,128)(2,1)S(1)}, bf16[768,768]{1,0:T(8,128)(2,1)}, u32[]{:S(2)}) copy-start(bf16[768,768]{1,0:T(8,128)(2,1)} %param.24) | copy-start | bytes 3538948
  7.2 55.3 %reduce-scatter.9.cloned.1.call-start = ((), (), s32[]{:S(2)}) async-start(), calls=%async_computation.11 | async-start | bytes 1966080 | tf_op jit(solution)/shard_map/reduce_scatter | solution.py:160
  19.8 13.9 %copy-start.28 = (bf16[512,192]{0,1:T(8,128)(2,1)}, bf16[512,192]{0,1:T(8,128)(2,1)S(1)}, u32[]{:S(2)}) copy-start(bf16[512,192]{0,1:T(8,128)(2,1)S(1)} %get-tuple-element.102) | copy-start | bytes 589828
  19.8 16.5 %copy-start.32 = (bf16[512,192]{0,1:T(8,128)(2,1)}, bf16[512,192]{0,1:T(8,128)(2,1)S(1)}, u32[]{:S(2)}) copy-start(bf16[512,192]{0,1:T(8,128)(2,1)S(1)} %get-tuple-element.101) | copy-start | bytes 589828
  23.9 16.9 %copy-start.15 = (bf16[1024,3,64]{0,2,1:T(8,128)(2,1)}, bf16[1024,3,64]{0,2,1:T(8,128)(2,1)S(1)}, u32[]{:S(2)}) copy-start(bf16[1024,3,64]{0,2,1:T(8,128)(2,1)S(1)} %get-tuple-element.113) | copy-start | bytes 1179652
  31.4 61.9 %reduce-scatter.13.cloned.1.call-start = ((), (), s32[]{:S(2)}) async-start(), calls=%async_computation.14 | async-start | bytes 1966080 | tf_op jit(solution)/shard_map/reduce_scatter | solution.py:160
  45.1 74.4 %all-gather.7.cloned.1.call-start = ((), (), s32[]{:S(2)}) async-start(), calls=%async_computation.15 | async-start | bytes 1966080 | tf_op jit(solution)/shard_map/all_gather | solution.py:168
  49.1 172.4 %copy-start.12 = (bf16[1,1024,768]{2,1,0:T(8,128)(2,1)}, bf16[1,1024,768]{2,1,0:T(8,128)(2,1)S(1)}, u32[]{:S(2)}) copy-start(bf16[1,1024,768]{2,1,0:T(8,128)(2,1)S(1)} %get-tuple-element.84) | copy-start | bytes 4718596
  62.5 34.8 %copy-start.7 = (bf16[256,768]{1,0:T(8,128)(2,1)S(1)}, bf16[256,768]{1,0:T(8,128)(2,1)}, u32[]{:S(2)}) copy-start(bf16[256,768]{1,0:T(8,128)(2,1)} %reduce-scatter.9.cloned.1.call-done) | copy-start | bytes 1179652
  99.7 41.5 %all-gather.5.cloned.1.call-start = ((), (), s32[]{:S(2)}) async-start(), calls=%async_computation.12 | async-start | bytes 1966080 | tf_op jit(solution)/shard_map/all_gather | solution.py:168
  100.3 90.4 %reduce-scatter.11.cloned.1.call-start = ((), (), s32[]{:S(2)}) async-start(), calls=%async_computation.13 | async-start | bytes 1966080 | tf_op jit(solution)/shard_map/reduce_scatter | solution.py:171
  141.2 18.6 %copy-start.111 = (bf16[768,768]{1,0:T(8,128)(2,1)S(1)}, bf16[768,768]{1,0:T(8,128)(2,1)}, u32[]{:S(2)}) copy-start(bf16[768,768]{1,0:T(8,128)(2,1)} %param.26) | copy-start | bytes 3538948
  162.4 59.1 %reduce-scatter.15.cloned.1.call-start = ((), (), s32[]{:S(2)}) async-start(), calls=%async_computation.16 | async-start | bytes 1966080 | tf_op jit(solution)/shard_map/reduce_scatter | solution.py:171
  166.8 133.3 %reduce-scatter.17.cloned.1.call-start = ((), (), s32[]{:S(2)}) async-start(), calls=%async_computation.17 | async-start | bytes 1966080 | tf_op jit(solution)/shard_map/reduce_scatter | solution.py:217
  229.5 8.6 %collective-permute-start = (bf16[256,768]{1,0:T(8,128)(2,1)}, bf16[256,768]{1,0:T(8,128)(2,1)}, u32[]{:S(2)}, u32[]{:S(2)}) collective-permute-start(bf16[256,768]{1,0:T(8,128)(2,1)} %get-tuple-element.73), channel_id=1, source_target_pairs={{0,1},{1,2},{2,3},{3,0},{4,5},{5,6},{6,7},{7,4},{8,9},{9,10},{10,1... | collective-permute-start | bytes 1179656 | tf_op jit(solution)/shard_map/ppermute | solution.py:191
  231.8 14.7 %collective-permute-start.3 = (bf16[256,768]{1,0:T(8,128)(2,1)}, bf16[256,768]{1,0:T(8,128)(2,1)}, u32[]{:S(2)}, u32[]{:S(2)}) collective-permute-start(bf16[256,768]{1,0:T(8,128)(2,1)} %get-tuple-element.69), channel_id=1, source_target_pairs={{0,1},{1,2},{2,3},{3,0},{4,5},{5,6},{6,7},{7,4},{8,9},{9,10},{10,1... | collective-permute-start | bytes 1179656 | tf_op jit(solution)/shard_map/ppermute | solution.py:191
  232.2 18.0 %collective-permute-start.1 = (bf16[256,768]{1,0:T(8,128)(2,1)}, bf16[256,768]{1,0:T(8,128)(2,1)}, u32[]{:S(2)}, u32[]{:S(2)}) collective-permute-start(bf16[256,768]{1,0:T(8,128)(2,1)} %get-tuple-element.73), channel_id=1, source_target_pairs={{0,3},{1,0},{2,1},{3,2},{4,7},{5,4},{6,5},{7,6},{8,11},{9,8},{10,9... | collective-permute-start | bytes 1179656 | tf_op jit(solution)/shard_map/ppermute | solution.py:196
  233.6 18.4 %collective-permute-start.4 = (bf16[256,768]{1,0:T(8,128)(2,1)}, bf16[256,768]{1,0:T(8,128)(2,1)}, u32[]{:S(2)}, u32[]{:S(2)}) collective-permute-start(bf16[256,768]{1,0:T(8,128)(2,1)} %get-tuple-element.69), channel_id=1, source_target_pairs={{0,3},{1,0},{2,1},{3,2},{4,7},{5,4},{6,5},{7,6},{8,11},{9,8},{10,9... | collective-permute-start | bytes 1179656 | tf_op jit(solution)/shard_map/ppermute | solution.py:196
  234.0 20.6 %copy-start.112 = (bf16[768,768]{1,0:T(8,128)(2,1)S(1)}, bf16[768,768]{1,0:T(8,128)(2,1)}, u32[]{:S(2)}) copy-start(bf16[768,768]{1,0:T(8,128)(2,1)} %param.26) | copy-start | bytes 3538948
  238.1 15.7 %collective-permute-start.2 = (bf16[256,768]{1,0:T(8,128)(2,1)}, bf16[256,768]{1,0:T(8,128)(2,1)S(1)}, u32[]{:S(2)}, u32[]{:S(2)}) collective-permute-start(bf16[256,768]{1,0:T(8,128)(2,1)} %collective-permute-done), channel_id=1, source_target_pairs={{0,1},{1,2},{2,3},{3,0},{4,5},{5,6},{6,7},{7,4},{8,9},{9,10},{10,1... | collective-permute-start | bytes 1179656 | tf_op jit(solution)/shard_map/ppermute | solution.py:191
  246.5 11.4 %collective-permute-start.5 = (bf16[256,768]{1,0:T(8,128)(2,1)}, bf16[256,768]{1,0:T(8,128)(2,1)S(1)}, u32[]{:S(2)}, u32[]{:S(2)}) collective-permute-start(bf16[256,768]{1,0:T(8,128)(2,1)} %collective-permute-done.3), channel_id=1, source_target_pairs={{0,1},{1,2},{2,3},{3,0},{4,5},{5,6},{6,7},{7,4},{8,9},{9,10},{10,1... | collective-permute-start | bytes 1179656 | tf_op jit(solution)/shard_map/ppermute | solution.py:191
  270.3 60.7 %reduce-scatter.21.cloned.1.call-start = ((), (), s32[]{:S(2)}) async-start(), calls=%async_computation.20 | async-start | bytes 1966080 | tf_op jit(solution)/shard_map/reduce_scatter | solution.py:217
  274.4 86.9 %all-gather.9.cloned.1.call-start = ((), (), s32[]{:S(2)}) async-start(), calls=%async_computation.18 | async-start | bytes 1966080 | tf_op jit(solution)/shard_map/all_gather | solution.py:231
  352.0 69.7 %all-to-all-start.2 = ((bf16[8,96,1536]{2,1,0:T(8,128)(2,1)}), bf16[8,96,1536]{2,1,0:T(8,128)(2,1)}, u32[]{:S(2)}, u32[]{:S(2)}) async-start(bf16[8,96,1536]{2,1,0:T(8,128)(2,1)} %bitcast.251), calls=%async_computation.10 | async-start | bytes 4718592 | tf_op jit(solution)/shard_map/all_to_all | solution.py:17
  357.7 23.6 %all-gather.11.cloned.1.call-start = ((), (), s32[]{:S(2)}) async-start(), calls=%async_computation.21 | async-start | bytes 1966080 | tf_op jit(solution)/shard_map/all_gather | solution.py:231
  361.0 162.8 %reduce-scatter.19.cloned.1.call-start = ((), (), s32[]{:S(2)}) async-start(), calls=%async_computation.19 | async-start | bytes 1966080 | tf_op jit(solution)/shard_map/reduce_scatter | solution.py:274
  397.8 127.2 %reduce-scatter.23.cloned.1.call-start = ((), (), s32[]{:S(2)}) async-start(), calls=%async_computation.22 | async-start | bytes 1966080 | tf_op jit(solution)/shard_map/reduce_scatter | solution.py:274
  421.7 15.7 %all-to-all-start.1 = ((bf16[8,24,768]{2,1,0:T(8,128)(2,1)}), bf16[8,24,768]{2,1,0:T(8,128)(2,1)}, u32[]{:S(2)}, u32[]{:S(2)}) async-start(bf16[8,24,768]{2,1,0:T(8,128)(2,1)} %bitcast.292), calls=%async_computation.9 | async-start | bytes 589824 | tf_op jit(solution)/shard_map/all_to_all | solution.py:17
  437.4 84.0 %all-to-all-start = ((bf16[8,96,3,192]{1,3,2,0:T(8,128)(2,1)}), bf16[8,96,3,192]{1,3,2,0:T(8,128)(2,1)}, u32[]{:S(2)}, u32[]{:S(2)}) async-start(bf16[8,96,3,192]{1,3,2,0:T(8,128)(2,1)} %copy.30), calls=%async_computation.8 | async-start | bytes 2359296 | tf_op jit(solution)/shard_map/all_to_all | solution.py:17
  492.4 31.4 %copy-start.14 = (f32[256,768]{1,0:T(8,128)S(1)}, f32[256,768]{1,0:T(8,128)}, u32[]{:S(2)}) copy-start(f32[256,768]{1,0:T(8,128)} %copy-done.13) | copy-start | bytes 2359300
  492.4 31.4 %copy-start.95 = (f32[256]{0:T(256)S(1)}, f32[256]{0:T(256)}, u32[]{:S(2)}) copy-start(f32[256]{0:T(256)} %copy-done.94) | copy-start | bytes 3076
  492.4 32.6 %copy-start.97 = (f32[256]{0:T(256)S(1)}, f32[256]{0:T(256)}, u32[]{:S(2)}) copy-start(f32[256]{0:T(256)} %copy-done.96) | copy-start | bytes 3076
  (122 other events, 462.6 us)
Sparse Core Ops, SparseCore 0:
  31.6 30.8 reduce-scatter.8
  65.2 28.1 reduce-scatter.12
  99.8 19.6 all-gather.6
  121.5 19.6 all-gather.4
  162.5 28.1 reduce-scatter.10
  193.3 28.1 reduce-scatter.14
  270.4 29.5 reduce-scatter.16
  302.8 28.1 reduce-scatter.20
  338.2 19.6 all-gather.8
  361.1 20.0 all-gather.10
  397.9 28.1 reduce-scatter.18
  428.7 28.6 reduce-scatter.22
